TPU v7x, 32 devices: a whole 2x2x4 slice. The times are simulated.
32 devices in a mesh: island: 8 (over z, x), fsdp: 4 (over y, core).
Axes of the slice: x: 2, y: 2, z: 4, core: 2. Of those that a mesh axis runs over, the one named last changes fastest.
Arguments:
- local_weights: bfloat16 [8, 4096, 512], P('island', 'fsdp'), may hold values from -6 to 6
- adam_first: bfloat16 [8, 4096, 512], P('island', 'fsdp'), may hold values from -6 to 6
- adam_second: bfloat16 [8, 4096, 512], P('island', 'fsdp'), may hold values from 0.5 to 4
- global_weights: float32 [4096, 512], P('fsdp'), may hold values from -6 to 6
- outer_momentum: float32 [4096, 512], P('fsdp'), may hold values from -3 to 3
- inputs: bfloat16 [8, 512, 4096], P('island', 'fsdp'), may hold values from -6 to 6
- key_cotangent: bfloat16 [8, 512, 512], P('island', 'fsdp'), may hold values from -24 to 24
Outputs:
- new_local: bfloat16 [8, 4096, 512], P('island', 'fsdp')
- new_first: bfloat16 [8, 4096, 512], P('island', 'fsdp')
- new_second: bfloat16 [8, 4096, 512], P('island', 'fsdp')
- new_global: float32 [4096, 512], P('fsdp')
- new_momentum: float32 [4096, 512], P('fsdp')
All inputs are finite; a program needn't handle non-finite values.
Results may differ from a plain program's by a relative error of at most 0.0065.
Values may be sent and summed in bfloat16 or wider, within the bound.
A program may use at most 64 MiB of HBM per device.

v0:
```python
import jax
import jax.numpy as jnp
from jax import lax
from jax.sharding import PartitionSpec as P

HEAD_DIM = 128


beta_one = 0.9
beta_two = 0.95
inner_rate = 0.02
weight_decay = 0.1
adam_epsilon = 1e-08
norm_epsilon = 1e-06
outer_rate = 0.7
outer_beta = 0.9
merge_weight = 0.5


def key_backward(keys, upstream):
    heads = keys.shape[1] // HEAD_DIM
    shaped = keys.reshape(keys.shape[0], heads, HEAD_DIM)
    cotan_heads = upstream.reshape(keys.shape[0], heads, HEAD_DIM)
    squares = jnp.mean(shaped * shaped, axis=-1, keepdims=True)
    inverse = lax.rsqrt(squares + norm_epsilon)
    normed = shaped * inverse
    projected = jnp.mean(cotan_heads * normed, axis=-1, keepdims=True)
    return (inverse * (cotan_heads - normed * projected)).reshape(keys.shape)


def local(
    local_weights, adam_first, adam_second, global_weights, outer_momentum, inputs, key_cotangent
):
    weights = local_weights[0]
    tokens = inputs[0]
    upstream = key_cotangent[0].astype(jnp.float32)
    scale = float(tokens.shape[1]) ** (-0.5)
    islands = lax.axis_size("island")
    summed = lax.psum(weights.astype(jnp.float32), "island")
    outer_grad = global_weights - summed / islands
    new_momentum = outer_beta * outer_momentum + outer_grad
    new_global = global_weights - outer_rate * (outer_grad + outer_beta * new_momentum)
    columns = tokens
    keys = (
        jnp.dot(
            columns,
            lax.all_gather(weights, "fsdp", axis=0, tiled=True),
            preferred_element_type=jnp.float32,
        )
        * scale
    )
    key_grad = (key_backward(keys, upstream) * scale).astype(jnp.bfloat16)
    columns = tokens
    gradient = lax.psum_scatter(
        lax.dot_general(
            columns, key_grad, (((0,), (0,)), ((), ())), preferred_element_type=jnp.float32
        ).astype(jnp.bfloat16),
        "fsdp",
        scatter_dimension=0,
        tiled=True,
    ).astype(jnp.float32)
    first_new = beta_one * adam_first[0].astype(jnp.float32) + (1.0 - beta_one) * gradient
    second_new = (
        beta_two * adam_second[0].astype(jnp.float32) + (1.0 - beta_two) * gradient * gradient
    )
    current = weights.astype(jnp.float32)
    inner = current - inner_rate * (
        first_new / (jnp.sqrt(second_new) + adam_epsilon) + weight_decay * current
    )
    merged = merge_weight * inner + (1.0 - merge_weight) * new_global
    return (
        merged.astype(jnp.bfloat16)[None],
        first_new.astype(jnp.bfloat16)[None],
        second_new.astype(jnp.bfloat16)[None],
        new_global,
        new_momentum,
    )


def solution(mesh):
    placed = (
        P("island", "fsdp", None),
        P("island", "fsdp", None),
        P("island", "fsdp", None),
        P("fsdp", None),
        P("fsdp", None),
        P("island", "fsdp", None),
        P("island", "fsdp", None),
    )
    return jax.shard_map(
        local,
        mesh=mesh,
        in_specs=placed,
        out_specs=(
            P("island", "fsdp", None),
            P("island", "fsdp", None),
            P("island", "fsdp", None),
            P("fsdp", None),
            P("fsdp", None),
        ),
        check_vma=False,
    )
```

profile of v0, /device:TPU:0, one launch (start us, length us, event | category | flops | bytes accessed | tf_op | source)
XLA Modules:
  0.0 142.2 jit_solution(9254017359627056663)
XLA Ops:
  8.0 0.0 copy-start
  8.0 0.0 all-gather.3.cloned.1.call-start
  8.1 0.7 all-gather.3.cloned.1.call-update
  8.7 0.0 all-reduce.2.cloned.1.call-start
  8.8 1.5 %copy.12 = bf16[1,1024,512]{1,2,0:T(8,128)(2,1)S(1)} copy(bf16[1,1024,512]{2,1,0:T(8,128)(2,1)} %param.7) | data formatting | bytes 2097152 | tf_op args[0]
  10.3 0.0 copy-start.3
  10.3 1.6 %bitcast_convert_fusion = f32[1024,512]{0,1:T(8,128)} fusion(bf16[1,1024,512]{1,2,0:T(8,128)(2,1)S(1)} %copy.12), kind=kLoop, calls=%fused_computation.17 | loop fusion | flops 524288 | bytes 3145728 | tf_op jit(solution)/shard_map/convert_element_type | solution.py:66
  11.9 0.0 all-reduce.2.cloned.1.call-update
  11.9 0.0 reduce-scatter.2.cloned.1.call-start
  12.0 0.0 copy-done.3
  12.0 0.1 reshape.52
  12.1 35.5 %all-gather.3.cloned.1.call-done = bf16[1,4096,512]{2,1,0:T(8,128)(2,1)} async-done(((bf16[1,1024,512]{2,1,0:T(8,128)(2,1)}), bf16[1,4096,512]{2,1,0:T(8,128)(2,1)}) %all-gather.3.cloned.1.call-update) | async-done | bytes 4194320 | tf_op jit(solution)/shard_map/all_gather | solution.py:47
  47.6 0.0 copy-done
  47.6 2.9 %fusion.7 = f32[128,512]{1,0:T(8,128)S(1)} fusion(bf16[1,4096,512]{2,1,0:T(8,128)(2,1)} %all-gather.3.cloned.1.call-done, bf16[1,128,4096]{2,1,0:T(8,128)(2,1)S(1)} %copy-done), kind=kOutput, calls=%fused_computation.14 | convolution fusion | flops 536936448 | bytes 5505024 | tf_op jit(solution)/shard_map/dot_general | solution.py:45
  50.5 0.1 reshape.50
  50.6 0.2 multiply_reduce_fusion.1
  50.8 0.4 multiply_reduce_fusion
  51.2 0.2 mul.112
  51.4 0.2 mul.107
  51.6 3.3 %fusion = bf16[4096,512]{0,1:T(8,128)(2,1)} fusion(bf16[1,128,4096]{2,1,0:T(8,128)(2,1)S(1)} %copy-done, f32[16,8,4,128]{3,2,1,0:T(4,128)S(1)} %bitcast.65, f32[128,512]{1,0:T(8,128)S(1)} %fusion.7, f32[16,8,4,128]{3,2,1,0:T(4,128)S(1)} %bitcast.66, bf16[1,128,512]{2,1,0:T(8,128)(2,1)S(1)} %copy-done.3), kind=kOutput, calls=%fused_computation.1 | convolution fusion | flops 539426816 | bytes 6160384 | tf_op jit(solution)/shard_map/dot_general | solution.py:55
  54.9 0.0 reduce-scatter.2.cloned.1.call-update
  54.9 2.9 %copy.16 = f32[1024,512]{0,1:T(8,128)} copy(f32[1024,512]{1,0:T(8,128)} %param.11) | data formatting | bytes 4194304 | tf_op args[4]
  57.8 2.9 %copy.17 = f32[1024,512]{0,1:T(8,128)} copy(f32[1024,512]{1,0:T(8,128)} %param.10) | data formatting | bytes 4194304 | tf_op args[3]
  60.7 1.5 %copy.13 = bf16[1,1024,512]{1,2,0:T(8,128)(2,1)S(1)} copy(bf16[1,1024,512]{2,1,0:T(8,128)(2,1)} %param.8) | data formatting | bytes 2097152 | tf_op args[1]
  62.3 2.5 %copy.14 = bf16[1,1024,512]{1,2,0:T(8,128)(2,1)} copy(bf16[1,1024,512]{2,1,0:T(8,128)(2,1)} %param.9) | data formatting | bytes 2097152 | tf_op args[2]
  64.8 52.7 %all-reduce.2.cloned.1.call-done = f32[1024,512]{0,1:T(8,128)} async-done(((f32[1024,512]{0,1:T(8,128)}), f32[1024,512]{0,1:T(8,128)}) %all-reduce.2.cloned.1.call-update) | async-done | bytes 2097168 | tf_op jit(solution)/shard_map/psum | solution.py:39
  117.5 0.0 reduce-scatter.2.cloned.1.call-done
  117.5 6.4 %fusion.14 = (bf16[1,1024,512]{1,2,0:T(8,128)(2,1)}, f32[1024,512]{0,1:T(8,128)}, f32[1024,512]{0,1:T(8,128)}, bf16[1,1024,512]{1,2,0:T(8,128)(2,1)}, bf16[1,1024,512]{1,2,0:T(8,128)(2,1)}) fusion(bf16[1,1024,512]{1,2,0:T(8,128)(2,1)} %copy.14, bf16[1024,512]{0,1:T(8,128)(2,1)} %reduce-scatter.2.cloned.1.call-done, bf16[1,1024,512]{1,2,0:T(8,128)(2,1)S(1)} %copy.13, ...), kind=kLoop, calls=%fused_computation.20 | loop fusion | flops 15728640 | bytes 17825792 | tf_op jit(solution)/shard_map/broadcast_in_dim | solution.py:72
  123.9 2.9 %copy.21 = f32[1024,512]{1,0:T(8,128)} copy(f32[1024,512]{0,1:T(8,128)} %get-tuple-element.11) | data formatting | bytes 4194304
  126.8 2.9 %copy.22 = f32[1024,512]{1,0:T(8,128)} copy(f32[1024,512]{0,1:T(8,128)} %get-tuple-element.12) | data formatting | bytes 4194304
  129.7 0.0 copy-start.2
  129.7 0.0 copy-start.1
  129.7 2.4 %copy.18 = bf16[1,1024,512]{2,1,0:T(8,128)(2,1)} copy(bf16[1,1024,512]{1,2,0:T(8,128)(2,1)} %get-tuple-element.10) | data formatting | bytes 2097152
  132.1 0.0 copy-done.2
  132.1 1.3 copy.19
  133.4 0.0 copy-done.1
  133.4 1.3 copy.20
  (2 shorter events, 0.0 us)
Async XLA Ops:
  8.0 39.6 %copy-start = (bf16[1,128,4096]{2,1,0:T(8,128)(2,1)S(1)}, bf16[1,128,4096]{2,1,0:T(8,128)(2,1)}, u32[]{:S(2)}) copy-start(bf16[1,128,4096]{2,1,0:T(8,128)(2,1)} %param.12) | copy-start | bytes 3145732
  8.0 39.6 %all-gather.3.cloned.1.call-start = ((), (), s32[]{:S(2)}) async-start(), calls=%async_computation.3 | async-start | bytes 5242880 | tf_op jit(solution)/shard_map/all_gather | solution.py:47
  8.7 108.8 %all-reduce.2.cloned.1.call-start = ((), (), s32[]{:S(2)}) async-start(), calls=%async_computation.2 | async-start | bytes 4194304 | tf_op jit(solution)/shard_map/psum | solution.py:39
  10.3 1.7 %copy-start.3 = (bf16[1,128,512]{2,1,0:T(8,128)(2,1)S(1)}, bf16[1,128,512]{2,1,0:T(8,128)(2,1)}, u32[]{:S(2)}) copy-start(bf16[1,128,512]{2,1,0:T(8,128)(2,1)} %param.13) | copy-start | bytes 393220
  11.9 105.6 %reduce-scatter.2.cloned.1.call-start = ((), (), s32[]{:S(2)}) async-start(), calls=%async_computation.1 | async-start | bytes 5242880 | tf_op jit(solution)/shard_map/reduce_scatter | solution.py:54
  129.7 2.4 %copy-start.2 = (bf16[1,1024,512]{1,2,0:T(8,128)(2,1)S(1)}, bf16[1,1024,512]{1,2,0:T(8,128)(2,1)}, u32[]{:S(2)}) copy-start(bf16[1,1024,512]{1,2,0:T(8,128)(2,1)} %get-tuple-element.14) | copy-start | bytes 3145732
  129.7 3.7 %copy-start.1 = (bf16[1,1024,512]{1,2,0:T(8,128)(2,1)S(1)}, bf16[1,1024,512]{1,2,0:T(8,128)(2,1)}, u32[]{:S(2)}) copy-start(bf16[1,1024,512]{1,2,0:T(8,128)(2,1)} %get-tuple-element.13) | copy-start | bytes 3145732
Sparse Core Ops, SparseCore 0:
  10.4 37.1 all-gather.2
  55.0 44.4 reduce-scatter.1
Sparse Core Ops, SparseCore 1:
  12.8 104.6 all-reduce.1
where the time goes:
time: 143 us; the launch traced here: 142 us
  waiting for transfers between devices  88.9 us (62%)
  local copies, waits for them, and re-layouts  22.8 us (16%)
  between operations  15.6 us (11%)
  other arithmetic  8.62 us (6%)
  matrix products  6.16 us (4%)
    psum x1, waiting for transfers between devices, local(): summed = lax.psum(weights.astype(jnp.float32), 'island')  52.7 us
    all_gather x1, waiting for transfers between devices, local(): lax.all_gather(weights, 'fsdp', axis=0, tiled=True)  35.5 us
    unnamed x18, local copies, waits for them, and re-layouts  22.2 us
    broadcast_in_dim x1, other arithmetic, local(): merged.astype(jnp.bfloat16)[None]  6.43 us
    dot_general x1, matrix products, local(): lax.dot_general(columns, key_grad, (((0,), (0,)), ((), ())), preferred_el...  3.25 us
    dot_general x1, matrix products, local(): jnp.dot(columns, lax.all_gather(weights, 'fsdp', axis=0, tiled=True), pre...  2.9 us
  transfers between devices with their start and end apart: 3, of which 2 were waited for; matrix products, arithmetic and copies ran while one was open for 14% of the time, Pallas kernels for 0%

commit v1 on v0

v1 whole, which is shorter than its diff:
```python
import functools

import jax
import jax.numpy as jnp
from jax import lax
from jax.experimental import pallas as pl
from jax.experimental.pallas import tpu as pltpu
from jax.sharding import PartitionSpec as P

HEAD_DIM = 128
MESH = pl.DeviceIdType.MESH

beta_one = 0.9
beta_two = 0.95
inner_rate = 0.02
weight_decay = 0.1
adam_epsilon = 1e-08
norm_epsilon = 1e-06
outer_rate = 0.7
outer_beta = 0.9
merge_weight = 0.5


def chunk_count(rows, islands):
    for chunks in (4, 2, 1):
        if islands % 2 == 0 and rows % (islands * chunks * 16) == 0:
            return chunks
    return 0


def head_backward(keys, upstream, scale):
    squares = jnp.mean(keys * keys, axis=-1, keepdims=True)
    inverse = lax.rsqrt(squares + norm_epsilon)
    normed = keys * inverse
    projected = jnp.mean(upstream * normed, axis=-1, keepdims=True)
    return (inverse * (upstream - normed * projected) * scale).astype(jnp.bfloat16)


def exchange(islands, shards, chunks, scale, *refs):
    w, x, cot = refs[:3]
    if chunks:
        (grad, mean, wp, xin, xp, psend, precv, kgin, kgp, kg, own,
         ysem, psem, ksem, csem, fsem, p1buf, part, p2buf, gathered,
         s1, s2, s3, s4) = refs[3:]
    else:
        (grad, wp, xin, xp, psend, precv, kgin, kgp, kg, own,
         ysem, psem, ksem, csem, fsem) = refs[3:]
    rows, width = w.shape
    chips = shards // 2
    island = lax.axis_index("island")
    shard = lax.axis_index("fsdp")
    core = lax.rem(shard, 2)
    chip = shard // 2
    partner = (island, chip * 2 + 1 - core)

    def peer(step):
        return (island, lax.rem(chip + step, chips) * 2 + core)

    def back(step):
        return (island, lax.rem(chip + chips - step, chips) * 2 + core)

    targets = [partner] + [peer(step) for step in range(1, chips)]
    if chunks:
        groups = islands // 2
        side = lax.rem(island, 2)
        line = island // 2
        across = (line * 2 + 1 - side, shard)

        def along(step):
            return (lax.rem(line + step, groups) * 2 + side, shard)

        targets += [across] + [along(step) for step in range(1, groups)]

    barrier = pltpu.get_barrier_semaphore()
    for target in targets:
        pl.semaphore_signal(barrier, inc=1, device_id=target, device_id_type=MESH)
    pl.semaphore_wait(barrier, len(targets))

    def remote(src, dst, sems, where, target):
        return pltpu.make_async_remote_copy(
            src_ref=src,
            dst_ref=dst,
            send_sem=sems.at[(0,) + where],
            recv_sem=sems.at[(1,) + where],
            device_id=target,
            device_id_type=MESH,
        )

    def columns(start):
        return pl.ds(pl.multiple_of(start, rows), rows)

    copies = []

    def begin(copy):
        copy.start()
        copies.append(copy)
        return copy

    y1 = []
    for step in range(1, chips):
        there = lax.rem(chip + step, chips)
        y1.append(begin(remote(
            x.at[:, pl.ds(pl.multiple_of(there * 2 * rows, 2 * rows), 2 * rows)],
            xin.at[step - 1], ysem, (step - 1,), peer(step))))
    if chunks:
        half = rows // 2
        size = half // chunks
        unit = size // groups
        p1 = [
            begin(remote(
                w.at[pl.ds(pl.multiple_of((1 - side) * half + q * size, size), size)],
                p1buf.at[q], s1, (q,), across))
            for q in range(chunks)
        ]
    wcopy = begin(remote(w, wp, csem, (0,), partner))
    xcopy = [begin(remote(
        x.at[:, columns((chip * 2 + 1 - core) * rows)], xp.at[0], csem, (1,), partner))]

    p2, p3, p4 = {}, {}, {}

    def pair_sum(q):
        p1[q].wait_recv()
        mine = w[pl.ds(pl.multiple_of(side * half + q * size, size), size), :]
        part[q] = (mine.astype(jnp.float32) + p1buf[q].astype(jnp.float32)).astype(jnp.bfloat16)
        for step in range(1, groups):
            there = lax.rem(line + step, groups)
            p2[q, step] = begin(remote(
                part.at[q, pl.ds(pl.multiple_of(there * unit, unit), unit)],
                p2buf.at[q, step - 1], s2, (q, step - 1), along(step)))

    def line_sum(q):
        total = part[q, pl.ds(pl.multiple_of(line * unit, unit), unit), :].astype(jnp.float32)
        for step in range(1, groups):
            p2[q, step].wait_recv()
            total += p2buf[q, step - 1].astype(jnp.float32)
        place = pl.ds(pl.multiple_of(side * half + q * size + line * unit, unit), unit)
        gathered[place, :] = (total / islands).astype(jnp.bfloat16)
        for step in range(1, groups):
            p3[q, step] = begin(remote(
                gathered.at[place], gathered.at[place], s3, (q, step - 1), along(step)))

    def return_half(q):
        for step in range(1, groups):
            p3[q, step].wait_recv()
        place = pl.ds(pl.multiple_of(side * half + q * size, size), size)
        p4[q] = begin(remote(gathered.at[place], gathered.at[place], s4, (q,), across))

    def product(left, right):
        return jnp.dot(left, right, preferred_element_type=jnp.float32)

    stages = []

    def advance(count):
        for _ in range(count):
            if stages:
                stage, q = stages.pop(0)
                stage(q)

    if chunks:
        for t in range(chunks + 4):
            if t < chunks:
                stages.append((pair_sum, t))
            if 0 <= t - 2 < chunks:
                stages.append((line_sum, t - 2))
            if 0 <= t - 4 < chunks:
                stages.append((return_half, t - 4))
    total_stages = len(stages)

    advance(2)
    wcopy.wait_recv()
    own[...] = product(x[:, columns(shard * rows)], w[...]) + product(
        x[:, columns((chip * 2 + 1 - core) * rows)], wp[...])
    advance(total_stages // 2 - 2)

    y3 = []
    for step in range(1, chips):
        y1[step - 1].wait_recv()
        xcopy.append(begin(remote(
            xin.at[step - 1, :, columns((1 - core) * rows)], xp.at[step], csem, (step + 1,), partner)))
        psend[step - 1] = product(xin[step - 1, :, columns(core * rows)], w[...]) + product(
            xin[step - 1, :, columns((1 - core) * rows)], wp[...])
        y3.append(begin(remote(
            psend.at[step - 1], precv.at[step - 1], psem, (step - 1,), back(step))))
    advance((total_stages - total_stages // 2) // 2)

    keys = own[...]
    for step in range(1, chips):
        y3[step - 1].wait_recv()
        keys += precv[step - 1]
    keys = keys * scale
    for head in range(width // HEAD_DIM):
        lanes = slice(head * HEAD_DIM, (head + 1) * HEAD_DIM)
        kg[:, lanes] = head_backward(keys[:, lanes], cot[:, lanes].astype(jnp.float32), scale)
    y4 = [
        begin(remote(kg, kgin.at[step - 1], ksem, (step - 1,), peer(step)))
        for step in range(1, chips)
    ]
    forwards = [begin(remote(kg, kgp.at[0], fsem, (0,), partner))]

    tile = min(256, rows)

    def add_block(read, upstream, first=False):
        @pl.loop(0, rows // tile)
        def _(t):
            start = pl.multiple_of(t * tile, tile)
            term = lax.dot_general(
                read(start), upstream[...], (((0,), (0,)), ((), ())),
                preferred_element_type=jnp.float32,
            ).astype(jnp.bfloat16).astype(jnp.float32)
            place = pl.ds(start, tile)
            grad[place, :] = term if first else grad[place, :] + term

    def lane(base):
        def at(start):
            return pl.ds(pl.multiple_of(base + start, tile), tile)
        return at

    mine = lane(shard * rows)
    add_block(lambda start: x[:, mine(start)], kg, first=True)
    forwards[0].wait_recv()
    xcopy[0].wait_recv()
    add_block(lambda start: xp[0, :, pl.ds(start, tile)], kgp.at[0])
    inner = lane(core * rows)
    for step in range(1, chips):
        y4[step - 1].wait_recv()
        forwards.append(begin(remote(
            kgin.at[step - 1], kgp.at[step], fsem, (step,), partner)))
        add_block(lambda start: xin[step - 1, :, inner(start)], kgin.at[step - 1])
    for step in range(1, chips):
        xcopy[step].wait_recv()
        forwards[step].wait_recv()
        add_block(lambda start: xp[step, :, pl.ds(start, tile)], kgp.at[step])
    advance(len(stages))
    if chunks:
        for q in range(chunks):
            p4[q].wait_recv()
        mean[...] = gathered[...]
    for copy in copies:
        copy.wait_send()


def local(
    local_weights, adam_first, adam_second, global_weights, outer_momentum, inputs, key_cotangent
):
    weights = local_weights[0]
    tokens = inputs[0]
    rows, width = weights.shape
    count, depth = tokens.shape
    scale = float(depth) ** (-0.5)
    islands, shards = lax.axis_size("island"), lax.axis_size("fsdp")
    chips = shards // 2
    others = max(chips - 1, 1)
    chunks = chunk_count(rows, islands)
    bf16, f32 = jnp.bfloat16, jnp.float32
    dma = pltpu.SemaphoreType.DMA
    out_shape = [jax.ShapeDtypeStruct((rows, width), f32)]
    scratch = [
        pltpu.VMEM((rows, width), bf16),
        pltpu.VMEM((others, count, 2 * rows), bf16),
        pltpu.VMEM((chips, count, rows), bf16),
        pltpu.VMEM((others, count, width), f32),
        pltpu.VMEM((others, count, width), f32),
        pltpu.VMEM((others, count, width), bf16),
        pltpu.VMEM((chips, count, width), bf16),
        pltpu.VMEM((count, width), bf16),
        pltpu.VMEM((count, width), f32),
        dma((2, others)),
        dma((2, others)),
        dma((2, others)),
        dma((2, chips + 1)),
        dma((2, chips)),
    ]
    if chunks:
        groups = islands // 2
        size = rows // 2 // chunks
        out_shape.append(jax.ShapeDtypeStruct((rows, width), bf16))
        scratch += [
            pltpu.VMEM((chunks, size, width), bf16),
            pltpu.VMEM((chunks, size, width), bf16),
            pltpu.VMEM((chunks, groups - 1, size // groups, width), bf16),
            pltpu.VMEM((rows, width), bf16),
            dma((2, chunks)),
            dma((2, chunks, groups - 1)),
            dma((2, chunks, groups - 1)),
            dma((2, chunks)),
        ]
    vmem = pl.BlockSpec(memory_space=pltpu.VMEM)
    results = pl.pallas_call(
        functools.partial(exchange, islands, shards, chunks, scale),
        out_shape=out_shape,
        in_specs=[vmem] * 3,
        out_specs=[vmem] * len(out_shape),
        scratch_shapes=scratch,
        compiler_params=pltpu.CompilerParams(
            collective_id=0, has_side_effects=True, vmem_limit_bytes=40 * 1024 * 1024
        ),
    )(weights, tokens, key_cotangent[0])
    gradient = results[0]
    if chunks:
        mean_local = results[1].astype(jnp.float32)
    else:
        mean_local = lax.psum(weights.astype(jnp.float32), "island") / islands
    outer_grad = global_weights - mean_local
    new_momentum = outer_beta * outer_momentum + outer_grad
    new_global = global_weights - outer_rate * (outer_grad + outer_beta * new_momentum)
    first_new = beta_one * adam_first[0].astype(jnp.float32) + (1.0 - beta_one) * gradient
    second_new = (
        beta_two * adam_second[0].astype(jnp.float32) + (1.0 - beta_two) * gradient * gradient
    )
    current = weights.astype(jnp.float32)
    inner = current - inner_rate * (
        first_new / (jnp.sqrt(second_new) + adam_epsilon) + weight_decay * current
    )
    merged = merge_weight * inner + (1.0 - merge_weight) * new_global
    return (
        merged.astype(jnp.bfloat16)[None],
        first_new.astype(jnp.bfloat16)[None],
        second_new.astype(jnp.bfloat16)[None],
        new_global,
        new_momentum,
    )


def solution(mesh):
    placed = (
        P("island", "fsdp", None),
        P("island", "fsdp", None),
        P("island", "fsdp", None),
        P("fsdp", None),
        P("fsdp", None),
        P("island", "fsdp", None),
        P("island", "fsdp", None),
    )
    return jax.shard_map(
        local,
        mesh=mesh,
        in_specs=placed,
        out_specs=(
            P("island", "fsdp", None),
            P("island", "fsdp", None),
            P("island", "fsdp", None),
            P("fsdp", None),
            P("fsdp", None),
        ),
        check_vma=False,
    )
```

time: 143 us -> 55.9 us (0.39)
  waiting for transfers between devices: 88.9 us -> 0 us
  Pallas kernels: 0 us -> 46.3 us
  local copies, waits for them, and re-layouts: 22.8 us -> 3.35 us
  between operations: 15.6 us -> 0.66 us
  matrix products: 6.16 us -> 0 us
  other arithmetic: 8.62 us -> 5.37 us
    psum x1 -> x0, waiting for transfers between devices: 52.7 us -> none  [local(): summed = lax.psum(weights.astype(jnp.float32), 'island')]
    pallas_call x0 -> x1, Pallas kernels: none -> 46.3 us  [local(): pl.pallas_call(functools.partial(exchange, islands, shards, chunks, scale...]
    all_gather x1 -> x0, waiting for transfers between devices: 35.5 us -> none  [local(): lax.all_gather(weights, 'fsdp', axis=0, tiled=True)]
    unnamed x18 -> x8, local copies, waits for them, and re-layouts: 22.2 us -> 3.35 us
    dot_general x2 -> x0, matrix products: 6.16 us -> none  [the longest x1 3.25 us: local(): lax.dot_general(columns, key_grad, (((0,), (0,)), ((), ())), preferred_el...]
    convert_element_type x1 -> x0, other arithmetic: 1.59 us -> none  [local(): current = weights.astype(jnp.float32)]
  transfers between devices with their start and end apart: 3 -> 0, of which waited for: 2 -> 0; matrix products, arithmetic and copies ran while one was open for 14% -> 0% of each run, Pallas kernels for 0% -> 0%
where the time goes in v1:
time: 55.9 us; the launch traced here: 55.6 us
  Pallas kernels  46.3 us (83%)
  other arithmetic  5.37 us (10%)
  local copies, waits for them, and re-layouts  3.35 us (6%)
  between operations  0.66 us (1%)
    pallas_call x1, Pallas kernels, local(): pl.pallas_call(functools.partial(exchange, islands, shards, chunks, scale...  46.3 us
    broadcast_in_dim x1, other arithmetic, local(): merged.astype(jnp.bfloat16)[None]  5.37 us
    unnamed x8, local copies, waits for them, and re-layouts  3.35 us

profile of v1, /device:TPU:0, one launch (start us, length us, event | category | flops | bytes accessed | tf_op | source)
XLA Modules:
  0.0 55.6 jit_solution(11302832739530170607)
XLA Ops:
  0.6 0.0 copy-start
  0.6 1.2 %copy-done = bf16[1,1024,512]{2,1,0:T(8,128)(2,1)S(1)} copy-done((bf16[1,1024,512]{2,1,0:T(8,128)(2,1)S(1)}, bf16[1,1024,512]{2,1,0:T(8,128)(2,1)}, u32[]{:S(2)}) %copy-start) | copy-done | bytes 1048600
  1.9 0.0 copy-start.1
  1.9 1.2 %copy-done.1 = bf16[1,128,4096]{2,1,0:T(8,128)(2,1)S(1)} copy-done((bf16[1,128,4096]{2,1,0:T(8,128)(2,1)S(1)}, bf16[1,128,4096]{2,1,0:T(8,128)(2,1)}, u32[]{:S(2)}) %copy-start.1) | copy-done | bytes 1048600
  3.1 0.0 copy-start.2
  3.1 0.9 %copy-done.2 = bf16[1,128,512]{2,1,0:T(8,128)(2,1)S(1)} copy-done((bf16[1,128,512]{2,1,0:T(8,128)(2,1)S(1)}, bf16[1,128,512]{2,1,0:T(8,128)(2,1)}, u32[]{:S(2)}) %copy-start.2) | copy-done | bytes 131096
  4.0 0.0 copy-start.3
  4.0 46.3 %shard_map.110 = (f32[1024,512]{1,0:T(8,128)S(1)}, bf16[1024,512]{1,0:T(8,128)(2,1)S(1)}) custom-call(bf16[1024,512]{1,0:T(8,128)(2,1)S(1)} %bitcast.30, bf16[128,4096]{1,0:T(8,128)(2,1)S(1)} %bitcast.31, bf16[128,512]{1,0:T(8,128)(2,1)S(1)} %bitcast.32), custom_call_target="tpu_custom_call" | custom-call | tf_op jit(solution)/shard_map/pallas_call | solution.py:288
  50.3 0.0 copy-done.3
  50.3 5.4 %fusion.10 = (bf16[1,1024,512]{2,1,0:T(8,128)(2,1)}, f32[1024,512]{1,0:T(8,128)}, f32[1024,512]{1,0:T(8,128)}, bf16[1,1024,512]{2,1,0:T(8,128)(2,1)}, bf16[1,1024,512]{2,1,0:T(8,128)(2,1)}) fusion(f32[1024,512]{1,0:T(8,128)S(1)} %get-tuple-element.7, bf16[1,1024,512]{2,1,0:T(8,128)(2,1)} %param.9, bf16[1,1024,512]{2,1,0:T(8,128)(2,1)} %param.8, ...), kind=kLoop, calls=%fused_computation.17 | loop fusion | flops 15204352 | bytes 17825792 | tf_op jit(solution)/shard_map/broadcast_in_dim | solution.py:316
Async XLA Ops:
  0.6 1.2 %copy-start = (bf16[1,1024,512]{2,1,0:T(8,128)(2,1)S(1)}, bf16[1,1024,512]{2,1,0:T(8,128)(2,1)}, u32[]{:S(2)}) copy-start(bf16[1,1024,512]{2,1,0:T(8,128)(2,1)} %param.7) | copy-start | bytes 3145732
  1.9 1.2 %copy-start.1 = (bf16[1,128,4096]{2,1,0:T(8,128)(2,1)S(1)}, bf16[1,128,4096]{2,1,0:T(8,128)(2,1)}, u32[]{:S(2)}) copy-start(bf16[1,128,4096]{2,1,0:T(8,128)(2,1)} %param.12) | copy-start | bytes 3145732
  3.1 0.9 %copy-start.2 = (bf16[1,128,512]{2,1,0:T(8,128)(2,1)S(1)}, bf16[1,128,512]{2,1,0:T(8,128)(2,1)}, u32[]{:S(2)}) copy-start(bf16[1,128,512]{2,1,0:T(8,128)(2,1)} %param.13) | copy-start | bytes 393220
  4.0 46.3 %copy-start.3 = (f32[1024,512]{1,0:T(8,128)S(1)}, f32[1024,512]{1,0:T(8,128)}, u32[]{:S(2)}) copy-start(f32[1024,512]{1,0:T(8,128)} %param.10) | copy-start | bytes 6291460

commit v2 on v1

--- a/solution.py
+++ b/solution.py
@@ -37,13 +37,13 @@
 
 
 def exchange(islands, shards, chunks, scale, *refs):
-    w, x, cot = refs[:3]
-    if chunks:
-        (grad, mean, wp, xin, xp, psend, precv, kgin, kgp, kg, own,
+    w_hbm, x_hbm, cot_hbm = refs[:3]
+    if chunks:
+        (grad, mean, w, x, cot, lsem, wp, xin, xp, psend, precv, kgin, kgp, kg, own,
          ysem, psem, ksem, csem, fsem, p1buf, part, p2buf, gathered,
          s1, s2, s3, s4) = refs[3:]
     else:
-        (grad, wp, xin, xp, psend, precv, kgin, kgp, kg, own,
+        (grad, w, x, cot, lsem, wp, xin, xp, psend, precv, kgin, kgp, kg, own,
          ysem, psem, ksem, csem, fsem) = refs[3:]
     rows, width = w.shape
     chips = shards // 2
@@ -70,6 +70,13 @@
             return (lax.rem(line + step, groups) * 2 + side, shard)
 
         targets += [across] + [along(step) for step in range(1, groups)]
+
+    loads = [
+        pltpu.make_async_copy(source, place, lsem.at[index])
+        for index, (source, place) in enumerate(((w_hbm, w), (x_hbm, x), (cot_hbm, cot)))
+    ]
+    for load in loads:
+        load.start()
 
     barrier = pltpu.get_barrier_semaphore()
     for target in targets:
@@ -100,7 +107,7 @@
     for step in range(1, chips):
         there = lax.rem(chip + step, chips)
         y1.append(begin(remote(
-            x.at[:, pl.ds(pl.multiple_of(there * 2 * rows, 2 * rows), 2 * rows)],
+            x_hbm.at[:, pl.ds(pl.multiple_of(there * 2 * rows, 2 * rows), 2 * rows)],
             xin.at[step - 1], ysem, (step - 1,), peer(step))))
     if chunks:
         half = rows // 2
@@ -108,13 +115,13 @@
         unit = size // groups
         p1 = [
             begin(remote(
-                w.at[pl.ds(pl.multiple_of((1 - side) * half + q * size, size), size)],
+                w_hbm.at[pl.ds(pl.multiple_of((1 - side) * half + q * size, size), size)],
                 p1buf.at[q], s1, (q,), across))
             for q in range(chunks)
         ]
-    wcopy = begin(remote(w, wp, csem, (0,), partner))
+    wcopy = begin(remote(w_hbm, wp, csem, (0,), partner))
     xcopy = [begin(remote(
-        x.at[:, columns((chip * 2 + 1 - core) * rows)], xp.at[0], csem, (1,), partner))]
+        x_hbm.at[:, columns((chip * 2 + 1 - core) * rows)], xp.at[0], csem, (1,), partner))]
 
     p2, p3, p4 = {}, {}, {}
 
@@ -149,44 +156,43 @@
         return jnp.dot(left, right, preferred_element_type=jnp.float32)
 
     stages = []
-
-    def advance(count):
-        for _ in range(count):
-            if stages:
-                stage, q = stages.pop(0)
+    for t in range(chunks + 3 if chunks else 0):
+        if t < chunks:
+            stages.append((pair_sum, t))
+        if 0 <= t - 3 < chunks:
+            stages.append((return_half, t - 3))
+        if 0 <= t - 1 < chunks:
+            stages.append((line_sum, t - 1))
+
+    def advance(last):
+        if last in stages:
+            for stage, q in stages[: stages.index(last) + 1]:
                 stage(q)
-
-    if chunks:
-        for t in range(chunks + 4):
-            if t < chunks:
-                stages.append((pair_sum, t))
-            if 0 <= t - 2 < chunks:
-                stages.append((line_sum, t - 2))
-            if 0 <= t - 4 < chunks:
-                stages.append((return_half, t - 4))
-    total_stages = len(stages)
-
-    advance(2)
+            del stages[: stages.index(last) + 1]
+
+    for load in loads:
+        load.wait()
+    advance((pair_sum, min(1, chunks - 1)))
     wcopy.wait_recv()
     own[...] = product(x[:, columns(shard * rows)], w[...]) + product(
         x[:, columns((chip * 2 + 1 - core) * rows)], wp[...])
-    advance(total_stages // 2 - 2)
+    advance((pair_sum, chunks - 1))
 
     y3 = []
     for step in range(1, chips):
         y1[step - 1].wait_recv()
         xcopy.append(begin(remote(
             xin.at[step - 1, :, columns((1 - core) * rows)], xp.at[step], csem, (step + 1,), partner)))
-        psend[step - 1] = product(xin[step - 1, :, columns(core * rows)], w[...]) + product(
-            xin[step - 1, :, columns((1 - core) * rows)], wp[...])
+        psend[step - 1] = (product(xin[step - 1, :, columns(core * rows)], w[...]) + product(
+            xin[step - 1, :, columns((1 - core) * rows)], wp[...])).astype(jnp.bfloat16)
         y3.append(begin(remote(
             psend.at[step - 1], precv.at[step - 1], psem, (step - 1,), back(step))))
-    advance((total_stages - total_stages // 2) // 2)
+    advance((line_sum, chunks - 1))
 
     keys = own[...]
     for step in range(1, chips):
         y3[step - 1].wait_recv()
-        keys += precv[step - 1]
+        keys += precv[step - 1].astype(jnp.float32)
     keys = keys * scale
     for head in range(width // HEAD_DIM):
         lanes = slice(head * HEAD_DIM, (head + 1) * HEAD_DIM)
@@ -220,17 +226,18 @@
     forwards[0].wait_recv()
     xcopy[0].wait_recv()
     add_block(lambda start: xp[0, :, pl.ds(start, tile)], kgp.at[0])
+    advance((return_half, chunks - 2))
     inner = lane(core * rows)
     for step in range(1, chips):
         y4[step - 1].wait_recv()
         forwards.append(begin(remote(
             kgin.at[step - 1], kgp.at[step], fsem, (step,), partner)))
         add_block(lambda start: xin[step - 1, :, inner(start)], kgin.at[step - 1])
+    advance((return_half, chunks - 1))
     for step in range(1, chips):
         xcopy[step].wait_recv()
         forwards[step].wait_recv()
         add_block(lambda start: xp[step, :, pl.ds(start, tile)], kgp.at[step])
-    advance(len(stages))
     if chunks:
         for q in range(chunks):
             p4[q].wait_recv()
@@ -256,10 +263,14 @@
     out_shape = [jax.ShapeDtypeStruct((rows, width), f32)]
     scratch = [
         pltpu.VMEM((rows, width), bf16),
+        pltpu.VMEM((count, depth), bf16),
+        pltpu.VMEM((count, width), bf16),
+        dma((3,)),
+        pltpu.VMEM((rows, width), bf16),
         pltpu.VMEM((others, count, 2 * rows), bf16),
         pltpu.VMEM((chips, count, rows), bf16),
-        pltpu.VMEM((others, count, width), f32),
-        pltpu.VMEM((others, count, width), f32),
+        pltpu.VMEM((others, count, width), bf16),
+        pltpu.VMEM((others, count, width), bf16),
         pltpu.VMEM((others, count, width), bf16),
         pltpu.VMEM((chips, count, width), bf16),
         pltpu.VMEM((count, width), bf16),
@@ -288,13 +299,13 @@
     results = pl.pallas_call(
         functools.partial(exchange, islands, shards, chunks, scale),
         out_shape=out_shape,
-        in_specs=[vmem] * 3,
+        in_specs=[pl.BlockSpec(memory_space=pltpu.HBM)] * 3,
         out_specs=[vmem] * len(out_shape),
         scratch_shapes=scratch,
         compiler_params=pltpu.CompilerParams(
             collective_id=0, has_side_effects=True, vmem_limit_bytes=40 * 1024 * 1024
         ),
-    )(weights, tokens, key_cotangent[0])
+    )(*(pltpu.with_memory_space_constraint(a, pltpu.HBM) for a in (weights, tokens, key_cotangent[0])))
     gradient = results[0]
     if chunks:
         mean_local = results[1].astype(jnp.float32)

time: 55.9 us -> 46.8 us (0.84)
  Pallas kernels: 46.3 us -> 40.5 us
  local copies, waits for them, and re-layouts: 3.35 us -> 0.01 us
    pallas_call x1, Pallas kernels: 46.3 us -> 40.5 us  [local(): pl.pallas_call(functools.partial(exchange, islands, shards, chunks, scale...]
    unnamed x8 -> x4, local copies, waits for them, and re-layouts: 3.35 us -> 0.01 us
where the time goes in v2:
time: 46.8 us; the launch traced here: 46.7 us
  Pallas kernels  40.5 us (87%)
  other arithmetic  5.53 us (12%)
  between operations  0.67 us (1%)
    pallas_call x1, Pallas kernels, local(): pl.pallas_call(functools.partial(exchange, islands, shards, chunks, scale...  40.5 us
    broadcast_in_dim x1, other arithmetic, local(): merged.astype(jnp.bfloat16)[None]  5.53 us

profile of v2, /device:TPU:0, one launch (start us, length us, event | category | flops | bytes accessed | tf_op | source)
XLA Modules:
  0.0 46.7 jit_solution(16126903886640570725)
XLA Ops:
  0.6 0.0 copy-start
  0.6 0.0 copy-start.1
  0.7 40.5 %shard_map.110 = (f32[1024,512]{1,0:T(8,128)S(1)}, bf16[1024,512]{1,0:T(8,128)(2,1)S(1)}) custom-call(bf16[1024,512]{1,0:T(8,128)(2,1)} %bitcast.30, bf16[128,4096]{1,0:T(8,128)(2,1)} %bitcast.31, bf16[128,512]{1,0:T(8,128)(2,1)} %bitcast.32), custom_call_target="tpu_custom_call" | custom-call | tf_op jit(solution)/shard_map/pallas_call | solution.py:299
  41.1 0.0 copy-done
  41.1 0.0 copy-done.1
  41.1 5.5 %fusion.10 = (bf16[1,1024,512]{2,1,0:T(8,128)(2,1)}, f32[1024,512]{1,0:T(8,128)}, f32[1024,512]{1,0:T(8,128)}, bf16[1,1024,512]{2,1,0:T(8,128)(2,1)}, bf16[1,1024,512]{2,1,0:T(8,128)(2,1)}) fusion(f32[1024,512]{1,0:T(8,128)S(1)} %get-tuple-element.7, bf16[1,1024,512]{2,1,0:T(8,128)(2,1)S(1)} %copy-done.1, bf16[1,1024,512]{2,1,0:T(8,128)(2,1)} %param.8, ...), kind=kLoop, calls=%fused_computation.17 | loop fusion | flops 15204352 | bytes 17825792 | tf_op jit(solution)/shard_map/broadcast_in_dim | solution.py:327
Async XLA Ops:
  0.6 40.5 %copy-start = (bf16[1,1024,512]{2,1,0:T(8,128)(2,1)S(1)}, bf16[1,1024,512]{2,1,0:T(8,128)(2,1)}, u32[]{:S(2)}) copy-start(bf16[1,1024,512]{2,1,0:T(8,128)(2,1)} %param.7) | copy-start | bytes 3145732
  0.6 40.5 %copy-start.1 = (bf16[1,1024,512]{2,1,0:T(8,128)(2,1)S(1)}, bf16[1,1024,512]{2,1,0:T(8,128)(2,1)}, u32[]{:S(2)}) copy-start(bf16[1,1024,512]{2,1,0:T(8,128)(2,1)} %param.9) | copy-start | bytes 3145732

commit v3 on v2

--- a/solution.py
+++ b/solution.py
@@ -22,8 +22,8 @@
 
 
 def chunk_count(rows, islands):
-    for chunks in (4, 2, 1):
-        if islands % 2 == 0 and rows % (islands * chunks * 16) == 0:
+    for chunks in (8, 4, 2, 1):
+        if islands & (islands - 1) == 0 and rows % (islands * chunks * 16) == 0:
             return chunks
     return 0
 
@@ -40,8 +40,7 @@
     w_hbm, x_hbm, cot_hbm = refs[:3]
     if chunks:
         (grad, mean, w, x, cot, lsem, wp, xin, xp, psend, precv, kgin, kgp, kg, own,
-         ysem, psem, ksem, csem, fsem, p1buf, part, p2buf, gathered,
-         s1, s2, s3, s4) = refs[3:]
+         ysem, psem, ksem, csem, fsem, landed, part, gathered, hsem) = refs[3:]
     else:
         (grad, w, x, cot, lsem, wp, xin, xp, psend, precv, kgin, kgp, kg, own,
          ysem, psem, ksem, csem, fsem) = refs[3:]
@@ -61,15 +60,10 @@
 
     targets = [partner] + [peer(step) for step in range(1, chips)]
     if chunks:
-        groups = islands // 2
-        side = lax.rem(island, 2)
-        line = island // 2
-        across = (line * 2 + 1 - side, shard)
-
-        def along(step):
-            return (lax.rem(line + step, groups) * 2 + side, shard)
-
-        targets += [across] + [along(step) for step in range(1, groups)]
+        levels = islands.bit_length() - 1
+        sides = [lax.rem(island // 2**bit, 2) for bit in range(levels)]
+        mates = [(island + (1 - 2 * sides[bit]) * 2**bit, shard) for bit in range(levels)]
+        targets += mates
 
     loads = [
         pltpu.make_async_copy(source, place, lsem.at[index])
@@ -109,74 +103,85 @@
         y1.append(begin(remote(
             x_hbm.at[:, pl.ds(pl.multiple_of(there * 2 * rows, 2 * rows), 2 * rows)],
             xin.at[step - 1], ysem, (step - 1,), peer(step))))
-    if chunks:
-        half = rows // 2
-        size = half // chunks
-        unit = size // groups
-        p1 = [
-            begin(remote(
-                w_hbm.at[pl.ds(pl.multiple_of((1 - side) * half + q * size, size), size)],
-                p1buf.at[q], s1, (q,), across))
+    halves, returns = {}, {}
+    if chunks:
+        span = rows // chunks
+        orders = [
+            [1, 0] + list(range(2, levels)) if levels > 1 and q % 2 == 1 else list(range(levels))
             for q in range(chunks)
         ]
+        starts = []
+        for q in range(chunks):
+            begins = [q * span]
+            for level, bit in enumerate(orders[q]):
+                begins.append(begins[level] + sides[bit] * (span >> (level + 1)))
+            starts.append(begins)
+
+    def segment(q, level):
+        return pl.ds(pl.multiple_of(starts[q][level], span >> level), span >> level)
+
+    def landing(level):
+        return pl.ds(span - (span >> level), span >> (level + 1))
+
+    def send_half(q, level):
+        bit, size = orders[q][level], span >> (level + 1)
+        away = starts[q][level] + (1 - sides[bit]) * size
+        source = part if level else w_hbm
+        halves[q, level] = begin(remote(
+            source.at[pl.ds(pl.multiple_of(away, size), size)],
+            landed.at[q, landing(level)], hsem, (q, level), mates[bit]))
+
+    def send_back(q, level):
+        place = segment(q, level + 1)
+        returns[q, level] = begin(remote(
+            gathered.at[place], gathered.at[place], hsem, (q, levels + level),
+            mates[orders[q][level]]))
+
+    for q in range(chunks):
+        send_half(q, 0)
     wcopy = begin(remote(w_hbm, wp, csem, (0,), partner))
     xcopy = [begin(remote(
         x_hbm.at[:, columns((chip * 2 + 1 - core) * rows)], xp.at[0], csem, (1,), partner))]
 
-    p2, p3, p4 = {}, {}, {}
-
-    def pair_sum(q):
-        p1[q].wait_recv()
-        mine = w[pl.ds(pl.multiple_of(side * half + q * size, size), size), :]
-        part[q] = (mine.astype(jnp.float32) + p1buf[q].astype(jnp.float32)).astype(jnp.bfloat16)
-        for step in range(1, groups):
-            there = lax.rem(line + step, groups)
-            p2[q, step] = begin(remote(
-                part.at[q, pl.ds(pl.multiple_of(there * unit, unit), unit)],
-                p2buf.at[q, step - 1], s2, (q, step - 1), along(step)))
-
-    def line_sum(q):
-        total = part[q, pl.ds(pl.multiple_of(line * unit, unit), unit), :].astype(jnp.float32)
-        for step in range(1, groups):
-            p2[q, step].wait_recv()
-            total += p2buf[q, step - 1].astype(jnp.float32)
-        place = pl.ds(pl.multiple_of(side * half + q * size + line * unit, unit), unit)
-        gathered[place, :] = (total / islands).astype(jnp.bfloat16)
-        for step in range(1, groups):
-            p3[q, step] = begin(remote(
-                gathered.at[place], gathered.at[place], s3, (q, step - 1), along(step)))
-
-    def return_half(q):
-        for step in range(1, groups):
-            p3[q, step].wait_recv()
-        place = pl.ds(pl.multiple_of(side * half + q * size, size), size)
-        p4[q] = begin(remote(gathered.at[place], gathered.at[place], s4, (q,), across))
+    def step_of(q, stage):
+        if stage < levels:
+            halves[q, stage].wait_recv()
+            place = segment(q, stage + 1)
+            held = (part if stage else w)[place, :].astype(jnp.float32)
+            total = held + landed[q, landing(stage), :].astype(jnp.float32)
+            if stage + 1 < levels:
+                part[place, :] = total.astype(jnp.bfloat16)
+                send_half(q, stage + 1)
+            else:
+                gathered[place, :] = (total / islands).astype(jnp.bfloat16)
+                send_back(q, levels - 1)
+        else:
+            level = 2 * levels - 1 - stage
+            returns[q, level].wait_recv()
+            if level:
+                send_back(q, level - 1)
 
     def product(left, right):
         return jnp.dot(left, right, preferred_element_type=jnp.float32)
 
     stages = []
-    for t in range(chunks + 3 if chunks else 0):
-        if t < chunks:
-            stages.append((pair_sum, t))
-        if 0 <= t - 3 < chunks:
-            stages.append((return_half, t - 3))
-        if 0 <= t - 1 < chunks:
-            stages.append((line_sum, t - 1))
-
-    def advance(last):
-        if last in stages:
-            for stage, q in stages[: stages.index(last) + 1]:
-                stage(q)
-            del stages[: stages.index(last) + 1]
+    for q in range(chunks):
+        for stage in range(2 * levels):
+            late = (q // 2) * 4.0 / chunks
+            stages.append((stage + late, q, stage))
+    stages.sort()
+
+    def advance(until):
+        while stages and stages[0][0] <= until:
+            step_of(*stages.pop(0)[1:])
 
     for load in loads:
         load.wait()
-    advance((pair_sum, min(1, chunks - 1)))
+    advance(0.5)
     wcopy.wait_recv()
     own[...] = product(x[:, columns(shard * rows)], w[...]) + product(
         x[:, columns((chip * 2 + 1 - core) * rows)], wp[...])
-    advance((pair_sum, chunks - 1))
+    advance(3.3)
 
     y3 = []
     for step in range(1, chips):
@@ -187,7 +192,7 @@
             xin[step - 1, :, columns((1 - core) * rows)], wp[...])).astype(jnp.bfloat16)
         y3.append(begin(remote(
             psend.at[step - 1], precv.at[step - 1], psem, (step - 1,), back(step))))
-    advance((line_sum, chunks - 1))
+    advance(5.1)
 
     keys = own[...]
     for step in range(1, chips):
@@ -226,21 +231,20 @@
     forwards[0].wait_recv()
     xcopy[0].wait_recv()
     add_block(lambda start: xp[0, :, pl.ds(start, tile)], kgp.at[0])
-    advance((return_half, chunks - 2))
+    advance(6.4)
     inner = lane(core * rows)
     for step in range(1, chips):
         y4[step - 1].wait_recv()
         forwards.append(begin(remote(
             kgin.at[step - 1], kgp.at[step], fsem, (step,), partner)))
         add_block(lambda start: xin[step - 1, :, inner(start)], kgin.at[step - 1])
-    advance((return_half, chunks - 1))
+    advance(6.9)
     for step in range(1, chips):
         xcopy[step].wait_recv()
         forwards[step].wait_recv()
         add_block(lambda start: xp[step, :, pl.ds(start, tile)], kgp.at[step])
-    if chunks:
-        for q in range(chunks):
-            p4[q].wait_recv()
+    advance(1000)
+    if chunks:
         mean[...] = gathered[...]
     for copy in copies:
         copy.wait_send()
@@ -282,18 +286,13 @@
         dma((2, chips)),
     ]
     if chunks:
-        groups = islands // 2
-        size = rows // 2 // chunks
+        levels = islands.bit_length() - 1
         out_shape.append(jax.ShapeDtypeStruct((rows, width), bf16))
         scratch += [
-            pltpu.VMEM((chunks, size, width), bf16),
-            pltpu.VMEM((chunks, size, width), bf16),
-            pltpu.VMEM((chunks, groups - 1, size // groups, width), bf16),
+            pltpu.VMEM((chunks, rows // chunks, width), bf16),
             pltpu.VMEM((rows, width), bf16),
-            dma((2, chunks)),
-            dma((2, chunks, groups - 1)),
-            dma((2, chunks, groups - 1)),
-            dma((2, chunks)),
+            pltpu.VMEM((rows, width), bf16),
+            dma((2, chunks, 2 * levels)),
         ]
     vmem = pl.BlockSpec(memory_space=pltpu.VMEM)
     results = pl.pallas_call(

time: 46.8 us -> 44.5 us (0.951)
  Pallas kernels: 40.5 us -> 38.1 us
    pallas_call x1, Pallas kernels: 40.5 us -> 38.1 us  [local(): pl.pallas_call(functools.partial(exchange, islands, shards, chunks, scale...]
where the time goes in v3:
time: 44.5 us; the launch traced here: 44.3 us
  Pallas kernels  38.1 us (86%)
  other arithmetic  5.53 us (12%)
  between operations  0.67 us (2%)
    pallas_call x1, Pallas kernels, local(): pl.pallas_call(functools.partial(exchange, islands, shards, chunks, scale...  38.1 us
    broadcast_in_dim x1, other arithmetic, local(): merged.astype(jnp.bfloat16)[None]  5.53 us

profile of v3, /device:TPU:0, one launch (start us, length us, event | category | flops | bytes accessed | tf_op | source)
XLA Modules:
  0.0 44.3 jit_solution(5446542955643380501)
XLA Ops:
  0.6 0.0 copy-start
  0.6 0.0 copy-start.1
  0.7 38.1 %shard_map.110 = (f32[1024,512]{1,0:T(8,128)S(1)}, bf16[1024,512]{1,0:T(8,128)(2,1)S(1)}) custom-call(bf16[1024,512]{1,0:T(8,128)(2,1)} %bitcast.30, bf16[128,4096]{1,0:T(8,128)(2,1)} %bitcast.31, bf16[128,512]{1,0:T(8,128)(2,1)} %bitcast.32), custom_call_target="tpu_custom_call" | custom-call | tf_op jit(solution)/shard_map/pallas_call | solution.py:298
  38.8 0.0 copy-done
  38.8 0.0 copy-done.1
  38.8 5.5 %fusion.10 = (bf16[1,1024,512]{2,1,0:T(8,128)(2,1)}, f32[1024,512]{1,0:T(8,128)}, f32[1024,512]{1,0:T(8,128)}, bf16[1,1024,512]{2,1,0:T(8,128)(2,1)}, bf16[1,1024,512]{2,1,0:T(8,128)(2,1)}) fusion(f32[1024,512]{1,0:T(8,128)S(1)} %get-tuple-element.7, bf16[1,1024,512]{2,1,0:T(8,128)(2,1)S(1)} %copy-done.1, bf16[1,1024,512]{2,1,0:T(8,128)(2,1)} %param.8, ...), kind=kLoop, calls=%fused_computation.17 | loop fusion | flops 15204352 | bytes 17825792 | tf_op jit(solution)/shard_map/broadcast_in_dim | solution.py:326
Async XLA Ops:
  0.6 38.2 %copy-start = (bf16[1,1024,512]{2,1,0:T(8,128)(2,1)S(1)}, bf16[1,1024,512]{2,1,0:T(8,128)(2,1)}, u32[]{:S(2)}) copy-start(bf16[1,1024,512]{2,1,0:T(8,128)(2,1)} %param.7) | copy-start | bytes 3145732
  0.6 38.2 %copy-start.1 = (bf16[1,1024,512]{2,1,0:T(8,128)(2,1)S(1)}, bf16[1,1024,512]{2,1,0:T(8,128)(2,1)}, u32[]{:S(2)}) copy-start(bf16[1,1024,512]{2,1,0:T(8,128)(2,1)} %param.9) | copy-start | bytes 3145732

commit v4 on v3

--- a/solution.py
+++ b/solution.py
@@ -167,7 +167,7 @@
     stages = []
     for q in range(chunks):
         for stage in range(2 * levels):
-            late = (q // 2) * 4.0 / chunks
+            late = (q // 2) * 6.0 / chunks
             stages.append((stage + late, q, stage))
     stages.sort()
 

time: 44.5 us -> 43.9 us (0.987)
  Pallas kernels: 38.1 us -> 37.6 us
    pallas_call x1, Pallas kernels: 38.1 us -> 37.6 us  [local(): pl.pallas_call(functools.partial(exchange, islands, shards, chunks, scale...]
where the time goes in v4:
time: 43.9 us; the launch traced here: 43.8 us
  Pallas kernels  37.6 us (86%)
  other arithmetic  5.53 us (13%)
  between operations  0.67 us (2%)
    pallas_call x1, Pallas kernels, local(): pl.pallas_call(functools.partial(exchange, islands, shards, chunks, scale...  37.6 us
    broadcast_in_dim x1, other arithmetic, local(): merged.astype(jnp.bfloat16)[None]  5.53 us

profile of v4, /device:TPU:0, one launch (start us, length us, event | category | flops | bytes accessed | tf_op | source)
XLA Modules:
  0.0 43.8 jit_solution(16846321739054371111)
XLA Ops:
  0.6 0.0 copy-start
  0.6 0.0 copy-start.1
  0.7 37.6 %shard_map.110 = (f32[1024,512]{1,0:T(8,128)S(1)}, bf16[1024,512]{1,0:T(8,128)(2,1)S(1)}) custom-call(bf16[1024,512]{1,0:T(8,128)(2,1)} %bitcast.30, bf16[128,4096]{1,0:T(8,128)(2,1)} %bitcast.31, bf16[128,512]{1,0:T(8,128)(2,1)} %bitcast.32), custom_call_target="tpu_custom_call" | custom-call | tf_op jit(solution)/shard_map/pallas_call | solution.py:298
  38.2 0.0 copy-done
  38.3 0.0 copy-done.1
  38.3 5.5 %fusion.10 = (bf16[1,1024,512]{2,1,0:T(8,128)(2,1)}, f32[1024,512]{1,0:T(8,128)}, f32[1024,512]{1,0:T(8,128)}, bf16[1,1024,512]{2,1,0:T(8,128)(2,1)}, bf16[1,1024,512]{2,1,0:T(8,128)(2,1)}) fusion(f32[1024,512]{1,0:T(8,128)S(1)} %get-tuple-element.7, bf16[1,1024,512]{2,1,0:T(8,128)(2,1)S(1)} %copy-done.1, bf16[1,1024,512]{2,1,0:T(8,128)(2,1)} %param.8, ...), kind=kLoop, calls=%fused_computation.17 | loop fusion | flops 15204352 | bytes 17825792 | tf_op jit(solution)/shard_map/broadcast_in_dim | solution.py:326
Async XLA Ops:
  0.6 37.6 %copy-start = (bf16[1,1024,512]{2,1,0:T(8,128)(2,1)S(1)}, bf16[1,1024,512]{2,1,0:T(8,128)(2,1)}, u32[]{:S(2)}) copy-start(bf16[1,1024,512]{2,1,0:T(8,128)(2,1)} %param.7) | copy-start | bytes 3145732
  0.6 37.6 %copy-start.1 = (bf16[1,1024,512]{2,1,0:T(8,128)(2,1)S(1)}, bf16[1,1024,512]{2,1,0:T(8,128)(2,1)}, u32[]{:S(2)}) copy-start(bf16[1,1024,512]{2,1,0:T(8,128)(2,1)} %param.9) | copy-start | bytes 3145732
